TPU v7x, 512 devices: a whole 4x4x16 slice. The times are simulated.
512 devices in a mesh: sec: 16 (over y, x), tile: 32 (over z, core).
Axes of the slice: x: 4, y: 4, z: 16, core: 2. Of those that a mesh axis runs over, the one named last changes fastest.
Arguments:
- beams: float32 [16, 2, 512, 2048], P('sec', None, 'tile'), may hold values from -6 to 6
- medium: float32 [16, 512, 2048], P('sec', 'tile'), may hold values from -0.3 to 0.3
Outputs:
- exit_fields: float32 [16, 2, 512, 2048], P('sec', None, 'tile')
All inputs are finite; a program needn't handle non-finite values.
Results may differ from a plain program's by a relative error of at most 0.00002.
Values sent between devices are 32-bit elements; how exact they have to be, the bound alone decides.
A program may use at most 64 MiB of HBM per device.

v0:
```python
import jax
import jax.numpy as jnp
from jax import lax
from jax.sharding import PartitionSpec as P

HALO = 4


diffract_coef = 0.5
step_length = 0.65


def padded_2(block, sides, width):
    for axis, dim in sides:
        count = lax.axis_size(axis)
        forward = [(i, i + 1) for i in range(count - 1)]
        backward = [(target, source) for source, target in forward]
        low = lax.ppermute(
            lax.slice_in_dim(block, block.shape[dim] - width, None, axis=dim), axis, forward
        )
        high = lax.ppermute(lax.slice_in_dim(block, 0, width, axis=dim), axis, backward)
        block = jnp.concatenate([low, block, high], axis=dim)
    return block


def laplace(envelope):
    pads = [(0, 0)] * (envelope.ndim - 2) + [(1, 1), (1, 1)]
    padded = jnp.pad(envelope, pads)
    return (
        padded[..., :-2, 1:-1]
        + padded[..., 2:, 1:-1]
        + padded[..., 1:-1, :-2]
        + padded[..., 1:-1, 2:]
        - 4.0 * envelope
    )


def derivative(envelope, medium_ext, inside):
    masked = envelope * inside
    forcing = diffract_coef * laplace(masked) + medium_ext * masked
    return jnp.stack([-forcing[..., 1, :, :], forcing[..., 0, :, :]], axis=-3)


def advance(envelope, medium_ext, inside):
    half_length = 0.5 * step_length
    slope_one = derivative(envelope, medium_ext, inside)
    slope_two = derivative(envelope + half_length * slope_one, medium_ext, inside)
    slope_three = derivative(envelope + half_length * slope_two, medium_ext, inside)
    slope_four = derivative(envelope + step_length * slope_three, medium_ext, inside)
    return envelope + step_length / 6.0 * (
        slope_one + 2.0 * slope_two + 2.0 * slope_three + slope_four
    )


def per_device(beams, medium):
    tile_rows = medium.shape[1]
    rim_depth = HALO
    tile_count = lax.axis_size("tile")
    tile_place = lax.axis_index("tile")
    global_row = (
        lax.broadcasted_iota(jnp.int32, (tile_rows + 2 * rim_depth, 1), 0)
        + tile_place * tile_rows
        - rim_depth
    )
    inside = ((global_row >= 0) & (global_row < tile_rows * tile_count)).astype(jnp.float32)
    medium_ext = padded_2(medium, (("tile", 1),), rim_depth)
    every_slab = lax.all_gather(medium_ext, "sec", axis=0, tiled=True)

    def section(envelope, slab_piece):
        widened = padded_2(envelope, (("tile", 1),), rim_depth)
        widened = advance(widened, slab_piece, inside)
        result = widened[:, rim_depth : rim_depth + tile_rows, :]
        return (result, None)

    final_field, unused = lax.scan(section, beams[0], every_slab)
    return final_field[None]


def solution(mesh):
    placed = (P("sec", None, "tile", None), P("sec", "tile", None))
    return jax.shard_map(
        per_device,
        mesh=mesh,
        in_specs=placed,
        out_specs=P("sec", None, "tile", None),
        check_vma=False,
    )
```

profile of v0, /device:TPU:128, one launch (start us, length us, event | category | flops | bytes accessed | tf_op | source)
XLA Modules:
  0.0 263.5 jit_solution(1515221760285659329)
XLA Ops:
  10.3 4.9 %collective-permute-start.3 = (f32[1,4,2048]{2,1,0:T(4,128)S(1)}, f32[1,4,2048]{2,1,0:T(4,128)S(1)}, u32[]{:S(2)}, u32[]{:S(2)}) collective-permute-start(f32[1,4,2048]{2,1,0:T(4,128)S(1)} %get-tuple-element.91), channel_id=1, source_target_pairs={{1,0},{2,1},{3,2},{4,3},{5,4},{6,5},{7,6},{8,7},{9,8},{10,9},{11,1... | collective-permute-start | bytes 98312 | tf_op jit(solution)/shard_map/ppermute | solution.py:21
  18.4 66.6 %all-gather.2.cloned.1.call-done = f32[16,24,2048]{2,1,0:T(8,128)} async-done(((f32[1,24,2048]{2,1,0:T(8,128)}), f32[16,24,2048]{2,1,0:T(8,128)}) %all-gather.2.cloned.1.call-update) | async-done | bytes 3145744 | tf_op jit(solution)/shard_map/all_gather | solution.py:67
  85.0 171.0 %while.13 = (s32[]{:T(128)}, f32[2,16,2048]{2,1,0:T(8,128)S(1)}, f32[16,24,2048]{2,1,0:T(8,128)}, s32[]{:T(128)}, s32[]{:T(128)}) while((s32[]{:T(128)}, f32[2,16,2048]{2,1,0:T(8,128)S(1)}, f32[16,24,2048]{2,1,0:T(8,128)}, s32[]{:T(128)}, s32[]{:T(128)}) %tuple.53), condition=%wide.region_1.2_spmd.clone, body=%wide.region_0.1_spmd.clone.sunk | while | flops 6127762 | bytes 15073917 | solution.py:75
  86.9 2.4 collective-permute-start.1
  90.3 3.4 %collective-permute-done.1 = f32[2,4,2048]{2,1,0:T(4,128)S(1)} collective-permute-done((f32[2,4,2048]{2,1,0:T(4,128)S(1)}, f32[2,4,2048]{2,1,0:T(4,128)S(1)}, u32[]{:S(2)}, u32[]{:S(2)}) %collective-permute-start.1) | collective-permute-done | bytes 65568 | tf_op jit(solution)/shard_map/while/body/eval_jaxpr/ppermute | solution.py:18
  97.6 2.4 collective-permute-start.1
  101.0 3.4 %collective-permute-done.1 = f32[2,4,2048]{2,1,0:T(4,128)S(1)} collective-permute-done((f32[2,4,2048]{2,1,0:T(4,128)S(1)}, f32[2,4,2048]{2,1,0:T(4,128)S(1)}, u32[]{:S(2)}, u32[]{:S(2)}) %collective-permute-start.1) | collective-permute-done | bytes 65568 | tf_op jit(solution)/shard_map/while/body/eval_jaxpr/ppermute | solution.py:18
  108.3 2.4 collective-permute-start.1
  111.7 3.4 %collective-permute-done.1 = f32[2,4,2048]{2,1,0:T(4,128)S(1)} collective-permute-done((f32[2,4,2048]{2,1,0:T(4,128)S(1)}, f32[2,4,2048]{2,1,0:T(4,128)S(1)}, u32[]{:S(2)}, u32[]{:S(2)}) %collective-permute-start.1) | collective-permute-done | bytes 65568 | tf_op jit(solution)/shard_map/while/body/eval_jaxpr/ppermute | solution.py:18
  119.0 2.4 collective-permute-start.1
  122.4 3.4 %collective-permute-done.1 = f32[2,4,2048]{2,1,0:T(4,128)S(1)} collective-permute-done((f32[2,4,2048]{2,1,0:T(4,128)S(1)}, f32[2,4,2048]{2,1,0:T(4,128)S(1)}, u32[]{:S(2)}, u32[]{:S(2)}) %collective-permute-start.1) | collective-permute-done | bytes 65568 | tf_op jit(solution)/shard_map/while/body/eval_jaxpr/ppermute | solution.py:18
  129.7 2.4 collective-permute-start.1
  133.1 3.4 %collective-permute-done.1 = f32[2,4,2048]{2,1,0:T(4,128)S(1)} collective-permute-done((f32[2,4,2048]{2,1,0:T(4,128)S(1)}, f32[2,4,2048]{2,1,0:T(4,128)S(1)}, u32[]{:S(2)}, u32[]{:S(2)}) %collective-permute-start.1) | collective-permute-done | bytes 65568 | tf_op jit(solution)/shard_map/while/body/eval_jaxpr/ppermute | solution.py:18
  143.8 3.4 %collective-permute-done.1 = f32[2,4,2048]{2,1,0:T(4,128)S(1)} collective-permute-done((f32[2,4,2048]{2,1,0:T(4,128)S(1)}, f32[2,4,2048]{2,1,0:T(4,128)S(1)}, u32[]{:S(2)}, u32[]{:S(2)}) %collective-permute-start.1) | collective-permute-done | bytes 65568 | tf_op jit(solution)/shard_map/while/body/eval_jaxpr/ppermute | solution.py:18
  154.4 3.4 %collective-permute-done.1 = f32[2,4,2048]{2,1,0:T(4,128)S(1)} collective-permute-done((f32[2,4,2048]{2,1,0:T(4,128)S(1)}, f32[2,4,2048]{2,1,0:T(4,128)S(1)}, u32[]{:S(2)}, u32[]{:S(2)}) %collective-permute-start.1) | collective-permute-done | bytes 65568 | tf_op jit(solution)/shard_map/while/body/eval_jaxpr/ppermute | solution.py:18
  165.1 3.4 %collective-permute-done.1 = f32[2,4,2048]{2,1,0:T(4,128)S(1)} collective-permute-done((f32[2,4,2048]{2,1,0:T(4,128)S(1)}, f32[2,4,2048]{2,1,0:T(4,128)S(1)}, u32[]{:S(2)}, u32[]{:S(2)}) %collective-permute-start.1) | collective-permute-done | bytes 65568 | tf_op jit(solution)/shard_map/while/body/eval_jaxpr/ppermute | solution.py:18
  175.8 3.4 %collective-permute-done.1 = f32[2,4,2048]{2,1,0:T(4,128)S(1)} collective-permute-done((f32[2,4,2048]{2,1,0:T(4,128)S(1)}, f32[2,4,2048]{2,1,0:T(4,128)S(1)}, u32[]{:S(2)}, u32[]{:S(2)}) %collective-permute-start.1) | collective-permute-done | bytes 65568 | tf_op jit(solution)/shard_map/while/body/eval_jaxpr/ppermute | solution.py:18
  186.5 3.4 %collective-permute-done.1 = f32[2,4,2048]{2,1,0:T(4,128)S(1)} collective-permute-done((f32[2,4,2048]{2,1,0:T(4,128)S(1)}, f32[2,4,2048]{2,1,0:T(4,128)S(1)}, u32[]{:S(2)}, u32[]{:S(2)}) %collective-permute-start.1) | collective-permute-done | bytes 65568 | tf_op jit(solution)/shard_map/while/body/eval_jaxpr/ppermute | solution.py:18
  197.2 3.4 %collective-permute-done.1 = f32[2,4,2048]{2,1,0:T(4,128)S(1)} collective-permute-done((f32[2,4,2048]{2,1,0:T(4,128)S(1)}, f32[2,4,2048]{2,1,0:T(4,128)S(1)}, u32[]{:S(2)}, u32[]{:S(2)}) %collective-permute-start.1) | collective-permute-done | bytes 65568 | tf_op jit(solution)/shard_map/while/body/eval_jaxpr/ppermute | solution.py:18
  207.9 3.4 %collective-permute-done.1 = f32[2,4,2048]{2,1,0:T(4,128)S(1)} collective-permute-done((f32[2,4,2048]{2,1,0:T(4,128)S(1)}, f32[2,4,2048]{2,1,0:T(4,128)S(1)}, u32[]{:S(2)}, u32[]{:S(2)}) %collective-permute-start.1) | collective-permute-done | bytes 65568 | tf_op jit(solution)/shard_map/while/body/eval_jaxpr/ppermute | solution.py:18
  218.6 3.4 %collective-permute-done.1 = f32[2,4,2048]{2,1,0:T(4,128)S(1)} collective-permute-done((f32[2,4,2048]{2,1,0:T(4,128)S(1)}, f32[2,4,2048]{2,1,0:T(4,128)S(1)}, u32[]{:S(2)}, u32[]{:S(2)}) %collective-permute-start.1) | collective-permute-done | bytes 65568 | tf_op jit(solution)/shard_map/while/body/eval_jaxpr/ppermute | solution.py:18
  229.3 3.4 %collective-permute-done.1 = f32[2,4,2048]{2,1,0:T(4,128)S(1)} collective-permute-done((f32[2,4,2048]{2,1,0:T(4,128)S(1)}, f32[2,4,2048]{2,1,0:T(4,128)S(1)}, u32[]{:S(2)}, u32[]{:S(2)}) %collective-permute-start.1) | collective-permute-done | bytes 65568 | tf_op jit(solution)/shard_map/while/body/eval_jaxpr/ppermute | solution.py:18
  240.0 3.4 %collective-permute-done.1 = f32[2,4,2048]{2,1,0:T(4,128)S(1)} collective-permute-done((f32[2,4,2048]{2,1,0:T(4,128)S(1)}, f32[2,4,2048]{2,1,0:T(4,128)S(1)}, u32[]{:S(2)}, u32[]{:S(2)}) %collective-permute-start.1) | collective-permute-done | bytes 65568 | tf_op jit(solution)/shard_map/while/body/eval_jaxpr/ppermute | solution.py:18
  250.7 3.4 %collective-permute-done.1 = f32[2,4,2048]{2,1,0:T(4,128)S(1)} collective-permute-done((f32[2,4,2048]{2,1,0:T(4,128)S(1)}, f32[2,4,2048]{2,1,0:T(4,128)S(1)}, u32[]{:S(2)}, u32[]{:S(2)}) %collective-permute-start.1) | collective-permute-done | bytes 65568 | tf_op jit(solution)/shard_map/while/body/eval_jaxpr/ppermute | solution.py:18
  (309 shorter events, 110.0 us)
Async XLA Ops:
  6.5 78.4 %all-gather.2.cloned.1.call-start = ((), (), s32[]{:S(2)}) async-start(), calls=%async_computation | async-start | bytes 3342336 | tf_op jit(solution)/shard_map/all_gather | solution.py:67
  8.4 6.8 %collective-permute-start.2 = (f32[1,4,2048]{2,1,0:T(4,128)S(1)}, f32[1,4,2048]{2,1,0:T(4,128)S(1)}, u32[]{:S(2)}, u32[]{:S(2)}) collective-permute-start(f32[1,4,2048]{2,1,0:T(4,128)S(1)} %get-tuple-element.90), channel_id=1, source_target_pairs={{0,1},{1,2},{2,3},{3,4},{4,5},{5,6},{6,7},{7,8},{8,9},{9,10},{10,1... | collective-permute-start | bytes 98312 | tf_op jit(solution)/shard_map/ppermute | solution.py:18
  10.3 6.4 %collective-permute-start.3 = (f32[1,4,2048]{2,1,0:T(4,128)S(1)}, f32[1,4,2048]{2,1,0:T(4,128)S(1)}, u32[]{:S(2)}, u32[]{:S(2)}) collective-permute-start(f32[1,4,2048]{2,1,0:T(4,128)S(1)} %get-tuple-element.91), channel_id=1, source_target_pairs={{1,0},{2,1},{3,2},{4,3},{5,4},{6,5},{7,6},{8,7},{9,8},{10,9},{11,1... | collective-permute-start | bytes 98312 | tf_op jit(solution)/shard_map/ppermute | solution.py:21
  85.0 5.3 %collective-permute-start = (f32[2,4,2048]{2,1,0:T(4,128)S(1)}, f32[2,4,2048]{2,1,0:T(4,128)S(1)}, u32[]{:S(2)}, u32[]{:S(2)}) collective-permute-start(f32[2,4,2048]{2,1,0:T(4,128)S(1)} %get-tuple-element.129), channel_id=1, source_target_pairs={{1,0},{2,1},{3,2},{4,3},{5,4},{6,5},{7,6},{8,7},{9,8},{10,9},{11,1... | collective-permute-start | bytes 196616 | tf_op jit(solution)/shard_map/while/body/eval_jaxpr/ppermute | solution.py:21
  86.9 6.8 %collective-permute-start.1 = (f32[2,4,2048]{2,1,0:T(4,128)S(1)}, f32[2,4,2048]{2,1,0:T(4,128)S(1)}, u32[]{:S(2)}, u32[]{:S(2)}) collective-permute-start(f32[2,4,2048]{2,1,0:T(4,128)S(1)} %get-tuple-element.130), channel_id=1, source_target_pairs={{0,1},{1,2},{2,3},{3,4},{4,5},{5,6},{6,7},{7,8},{8,9},{9,10},{10,1... | collective-permute-start | bytes 196616 | tf_op jit(solution)/shard_map/while/body/eval_jaxpr/ppermute | solution.py:18
  95.7 5.3 %collective-permute-start = (f32[2,4,2048]{2,1,0:T(4,128)S(1)}, f32[2,4,2048]{2,1,0:T(4,128)S(1)}, u32[]{:S(2)}, u32[]{:S(2)}) collective-permute-start(f32[2,4,2048]{2,1,0:T(4,128)S(1)} %get-tuple-element.129), channel_id=1, source_target_pairs={{1,0},{2,1},{3,2},{4,3},{5,4},{6,5},{7,6},{8,7},{9,8},{10,9},{11,1... | collective-permute-start | bytes 196616 | tf_op jit(solution)/shard_map/while/body/eval_jaxpr/ppermute | solution.py:21
  97.6 6.8 %collective-permute-start.1 = (f32[2,4,2048]{2,1,0:T(4,128)S(1)}, f32[2,4,2048]{2,1,0:T(4,128)S(1)}, u32[]{:S(2)}, u32[]{:S(2)}) collective-permute-start(f32[2,4,2048]{2,1,0:T(4,128)S(1)} %get-tuple-element.130), channel_id=1, source_target_pairs={{0,1},{1,2},{2,3},{3,4},{4,5},{5,6},{6,7},{7,8},{8,9},{9,10},{10,1... | collective-permute-start | bytes 196616 | tf_op jit(solution)/shard_map/while/body/eval_jaxpr/ppermute | solution.py:18
  106.4 5.3 %collective-permute-start = (f32[2,4,2048]{2,1,0:T(4,128)S(1)}, f32[2,4,2048]{2,1,0:T(4,128)S(1)}, u32[]{:S(2)}, u32[]{:S(2)}) collective-permute-start(f32[2,4,2048]{2,1,0:T(4,128)S(1)} %get-tuple-element.129), channel_id=1, source_target_pairs={{1,0},{2,1},{3,2},{4,3},{5,4},{6,5},{7,6},{8,7},{9,8},{10,9},{11,1... | collective-permute-start | bytes 196616 | tf_op jit(solution)/shard_map/while/body/eval_jaxpr/ppermute | solution.py:21
  108.3 6.8 %collective-permute-start.1 = (f32[2,4,2048]{2,1,0:T(4,128)S(1)}, f32[2,4,2048]{2,1,0:T(4,128)S(1)}, u32[]{:S(2)}, u32[]{:S(2)}) collective-permute-start(f32[2,4,2048]{2,1,0:T(4,128)S(1)} %get-tuple-element.130), channel_id=1, source_target_pairs={{0,1},{1,2},{2,3},{3,4},{4,5},{5,6},{6,7},{7,8},{8,9},{9,10},{10,1... | collective-permute-start | bytes 196616 | tf_op jit(solution)/shard_map/while/body/eval_jaxpr/ppermute | solution.py:18
  117.1 5.3 %collective-permute-start = (f32[2,4,2048]{2,1,0:T(4,128)S(1)}, f32[2,4,2048]{2,1,0:T(4,128)S(1)}, u32[]{:S(2)}, u32[]{:S(2)}) collective-permute-start(f32[2,4,2048]{2,1,0:T(4,128)S(1)} %get-tuple-element.129), channel_id=1, source_target_pairs={{1,0},{2,1},{3,2},{4,3},{5,4},{6,5},{7,6},{8,7},{9,8},{10,9},{11,1... | collective-permute-start | bytes 196616 | tf_op jit(solution)/shard_map/while/body/eval_jaxpr/ppermute | solution.py:21
  119.0 6.8 %collective-permute-start.1 = (f32[2,4,2048]{2,1,0:T(4,128)S(1)}, f32[2,4,2048]{2,1,0:T(4,128)S(1)}, u32[]{:S(2)}, u32[]{:S(2)}) collective-permute-start(f32[2,4,2048]{2,1,0:T(4,128)S(1)} %get-tuple-element.130), channel_id=1, source_target_pairs={{0,1},{1,2},{2,3},{3,4},{4,5},{5,6},{6,7},{7,8},{8,9},{9,10},{10,1... | collective-permute-start | bytes 196616 | tf_op jit(solution)/shard_map/while/body/eval_jaxpr/ppermute | solution.py:18
  127.8 5.3 %collective-permute-start = (f32[2,4,2048]{2,1,0:T(4,128)S(1)}, f32[2,4,2048]{2,1,0:T(4,128)S(1)}, u32[]{:S(2)}, u32[]{:S(2)}) collective-permute-start(f32[2,4,2048]{2,1,0:T(4,128)S(1)} %get-tuple-element.129), channel_id=1, source_target_pairs={{1,0},{2,1},{3,2},{4,3},{5,4},{6,5},{7,6},{8,7},{9,8},{10,9},{11,1... | collective-permute-start | bytes 196616 | tf_op jit(solution)/shard_map/while/body/eval_jaxpr/ppermute | solution.py:21
  129.7 6.8 %collective-permute-start.1 = (f32[2,4,2048]{2,1,0:T(4,128)S(1)}, f32[2,4,2048]{2,1,0:T(4,128)S(1)}, u32[]{:S(2)}, u32[]{:S(2)}) collective-permute-start(f32[2,4,2048]{2,1,0:T(4,128)S(1)} %get-tuple-element.130), channel_id=1, source_target_pairs={{0,1},{1,2},{2,3},{3,4},{4,5},{5,6},{6,7},{7,8},{8,9},{9,10},{10,1... | collective-permute-start | bytes 196616 | tf_op jit(solution)/shard_map/while/body/eval_jaxpr/ppermute | solution.py:18
  140.4 6.8 %collective-permute-start.1 = (f32[2,4,2048]{2,1,0:T(4,128)S(1)}, f32[2,4,2048]{2,1,0:T(4,128)S(1)}, u32[]{:S(2)}, u32[]{:S(2)}) collective-permute-start(f32[2,4,2048]{2,1,0:T(4,128)S(1)} %get-tuple-element.130), channel_id=1, source_target_pairs={{0,1},{1,2},{2,3},{3,4},{4,5},{5,6},{6,7},{7,8},{8,9},{9,10},{10,1... | collective-permute-start | bytes 196616 | tf_op jit(solution)/shard_map/while/body/eval_jaxpr/ppermute | solution.py:18
  151.1 6.8 %collective-permute-start.1 = (f32[2,4,2048]{2,1,0:T(4,128)S(1)}, f32[2,4,2048]{2,1,0:T(4,128)S(1)}, u32[]{:S(2)}, u32[]{:S(2)}) collective-permute-start(f32[2,4,2048]{2,1,0:T(4,128)S(1)} %get-tuple-element.130), channel_id=1, source_target_pairs={{0,1},{1,2},{2,3},{3,4},{4,5},{5,6},{6,7},{7,8},{8,9},{9,10},{10,1... | collective-permute-start | bytes 196616 | tf_op jit(solution)/shard_map/while/body/eval_jaxpr/ppermute | solution.py:18
  161.7 6.8 %collective-permute-start.1 = (f32[2,4,2048]{2,1,0:T(4,128)S(1)}, f32[2,4,2048]{2,1,0:T(4,128)S(1)}, u32[]{:S(2)}, u32[]{:S(2)}) collective-permute-start(f32[2,4,2048]{2,1,0:T(4,128)S(1)} %get-tuple-element.130), channel_id=1, source_target_pairs={{0,1},{1,2},{2,3},{3,4},{4,5},{5,6},{6,7},{7,8},{8,9},{9,10},{10,1... | collective-permute-start | bytes 196616 | tf_op jit(solution)/shard_map/while/body/eval_jaxpr/ppermute | solution.py:18
  172.4 6.8 %collective-permute-start.1 = (f32[2,4,2048]{2,1,0:T(4,128)S(1)}, f32[2,4,2048]{2,1,0:T(4,128)S(1)}, u32[]{:S(2)}, u32[]{:S(2)}) collective-permute-start(f32[2,4,2048]{2,1,0:T(4,128)S(1)} %get-tuple-element.130), channel_id=1, source_target_pairs={{0,1},{1,2},{2,3},{3,4},{4,5},{5,6},{6,7},{7,8},{8,9},{9,10},{10,1... | collective-permute-start | bytes 196616 | tf_op jit(solution)/shard_map/while/body/eval_jaxpr/ppermute | solution.py:18
  183.1 6.8 %collective-permute-start.1 = (f32[2,4,2048]{2,1,0:T(4,128)S(1)}, f32[2,4,2048]{2,1,0:T(4,128)S(1)}, u32[]{:S(2)}, u32[]{:S(2)}) collective-permute-start(f32[2,4,2048]{2,1,0:T(4,128)S(1)} %get-tuple-element.130), channel_id=1, source_target_pairs={{0,1},{1,2},{2,3},{3,4},{4,5},{5,6},{6,7},{7,8},{8,9},{9,10},{10,1... | collective-permute-start | bytes 196616 | tf_op jit(solution)/shard_map/while/body/eval_jaxpr/ppermute | solution.py:18
  193.8 6.8 %collective-permute-start.1 = (f32[2,4,2048]{2,1,0:T(4,128)S(1)}, f32[2,4,2048]{2,1,0:T(4,128)S(1)}, u32[]{:S(2)}, u32[]{:S(2)}) collective-permute-start(f32[2,4,2048]{2,1,0:T(4,128)S(1)} %get-tuple-element.130), channel_id=1, source_target_pairs={{0,1},{1,2},{2,3},{3,4},{4,5},{5,6},{6,7},{7,8},{8,9},{9,10},{10,1... | collective-permute-start | bytes 196616 | tf_op jit(solution)/shard_map/while/body/eval_jaxpr/ppermute | solution.py:18
  204.5 6.8 %collective-permute-start.1 = (f32[2,4,2048]{2,1,0:T(4,128)S(1)}, f32[2,4,2048]{2,1,0:T(4,128)S(1)}, u32[]{:S(2)}, u32[]{:S(2)}) collective-permute-start(f32[2,4,2048]{2,1,0:T(4,128)S(1)} %get-tuple-element.130), channel_id=1, source_target_pairs={{0,1},{1,2},{2,3},{3,4},{4,5},{5,6},{6,7},{7,8},{8,9},{9,10},{10,1... | collective-permute-start | bytes 196616 | tf_op jit(solution)/shard_map/while/body/eval_jaxpr/ppermute | solution.py:18
  215.2 6.8 %collective-permute-start.1 = (f32[2,4,2048]{2,1,0:T(4,128)S(1)}, f32[2,4,2048]{2,1,0:T(4,128)S(1)}, u32[]{:S(2)}, u32[]{:S(2)}) collective-permute-start(f32[2,4,2048]{2,1,0:T(4,128)S(1)} %get-tuple-element.130), channel_id=1, source_target_pairs={{0,1},{1,2},{2,3},{3,4},{4,5},{5,6},{6,7},{7,8},{8,9},{9,10},{10,1... | collective-permute-start | bytes 196616 | tf_op jit(solution)/shard_map/while/body/eval_jaxpr/ppermute | solution.py:18
  225.9 6.8 %collective-permute-start.1 = (f32[2,4,2048]{2,1,0:T(4,128)S(1)}, f32[2,4,2048]{2,1,0:T(4,128)S(1)}, u32[]{:S(2)}, u32[]{:S(2)}) collective-permute-start(f32[2,4,2048]{2,1,0:T(4,128)S(1)} %get-tuple-element.130), channel_id=1, source_target_pairs={{0,1},{1,2},{2,3},{3,4},{4,5},{5,6},{6,7},{7,8},{8,9},{9,10},{10,1... | collective-permute-start | bytes 196616 | tf_op jit(solution)/shard_map/while/body/eval_jaxpr/ppermute | solution.py:18
  236.6 6.8 %collective-permute-start.1 = (f32[2,4,2048]{2,1,0:T(4,128)S(1)}, f32[2,4,2048]{2,1,0:T(4,128)S(1)}, u32[]{:S(2)}, u32[]{:S(2)}) collective-permute-start(f32[2,4,2048]{2,1,0:T(4,128)S(1)} %get-tuple-element.130), channel_id=1, source_target_pairs={{0,1},{1,2},{2,3},{3,4},{4,5},{5,6},{6,7},{7,8},{8,9},{9,10},{10,1... | collective-permute-start | bytes 196616 | tf_op jit(solution)/shard_map/while/body/eval_jaxpr/ppermute | solution.py:18
  247.3 6.8 %collective-permute-start.1 = (f32[2,4,2048]{2,1,0:T(4,128)S(1)}, f32[2,4,2048]{2,1,0:T(4,128)S(1)}, u32[]{:S(2)}, u32[]{:S(2)}) collective-permute-start(f32[2,4,2048]{2,1,0:T(4,128)S(1)} %get-tuple-element.130), channel_id=1, source_target_pairs={{0,1},{1,2},{2,3},{3,4},{4,5},{5,6},{6,7},{7,8},{8,9},{9,10},{10,1... | collective-permute-start | bytes 196616 | tf_op jit(solution)/shard_map/while/body/eval_jaxpr/ppermute | solution.py:18
  (12 other events, 59.1 us)
Sparse Core Ops, SparseCore 0:
  18.5 66.4 all-gather.1
where the time goes:
time: 265 us; the launch traced here: 264 us
  waiting for transfers between devices  123 us (46%)
  starting transfers between devices  76 us (29%)
  other arithmetic  31.2 us (12%)
  local copies, waits for them, and re-layouts  18 us (7%)
  between operations  13.4 us (5%)
    all_gather x1, waiting for transfers between devices, per_device(): every_slab = lax.all_gather(medium_ext, 'sec', axis=0, tiled=True)  66.6 us
    ppermute x17, waiting for transfers between devices, padded_2(): lax.ppermute(lax.slice_in_dim(block, block.shape[dim] - width, None, axis...  54.5 us
    ppermute x17, starting transfers between devices, padded_2(): lax.ppermute(lax.slice_in_dim(block, block.shape[dim] - width, None, axis...  40.4 us
    ppermute x17, starting transfers between devices, padded_2(): lax.ppermute(lax.slice_in_dim(block, 0, width, axis=dim), axis, backward)  35.6 us
    add x64, other arithmetic, derivative(): forcing = diffract_coef * laplace(masked) + medium_ext * masked  17.6 us
    mul x16, local copies, waits for them, and re-layouts, derivative(): forcing = diffract_coef * laplace(masked) + medium_ext * masked  15.1 us
    mul x80, other arithmetic, derivative(): masked = envelope * inside  7.17 us
  transfers between devices with their start and end apart: 35, of which 18 were waited for; matrix products, arithmetic and copies ran while one was open for 6% of the time, Pallas kernels for 0%

commit v1 on v0

v1 whole, which is shorter than its diff:
```python
import functools

import jax
import jax.numpy as jnp
from jax import lax
from jax.experimental import pallas as pl
from jax.experimental.pallas import tpu as pltpu
from jax.sharding import PartitionSpec as P

MESH = pl.DeviceIdType.MESH
STEP = 0.65
DIFFRACT = 0.5
SCALES = tuple(DIFFRACT * STEP / d for d in (4.0, 3.0, 2.0, 1.0))
GROUP = 4
PANELS = 16
LANES = 128
UNROLL = 4


def swap_bits(tiles):
    lane = lax.broadcasted_iota(jnp.int32, tiles[0].shape, len(tiles[0].shape) - 1)
    axis = len(tiles[0].shape) - 1
    tiles = list(tiles)
    for bit in range(4):
        low = (lane & (1 << bit)) == 0
        for i in range(PANELS):
            if i & (1 << bit):
                continue
            j = i | (1 << bit)
            x, y = tiles[i], tiles[j]
            tiles[i] = jnp.where(low, x, pltpu.roll(y, 1 << bit, axis))
            tiles[j] = jnp.where(low, pltpu.roll(x, LANES - (1 << bit), axis), y)
    return tiles


def kernel(tiles, secs, beams, medium, out, field, work, index, scale, m_send, m_recv, h_send, h_recv, f_send, f_recv):
    rows = medium.shape[1]
    ext = 3 * rows
    pad = 8
    me = lax.axis_index("sec")
    t = lax.axis_index("tile")
    odd = lax.rem(t, 2)
    y, x = lax.div(me, 4), lax.rem(me, 4)
    a = x * (1 - odd) + y * odd
    b = y * (1 - odd) + x * odd

    def sid(da, db):
        return lax.rem(a + da, 4) * (1 + 3 * odd) + lax.rem(b + db, 4) * (4 - 3 * odd)

    has_up = t > 0
    has_down = t < tiles - 1

    barrier = pltpu.get_barrier_semaphore()
    for peer in (sid(1, 0), sid(3, 0), sid(0, 1), sid(0, 3)):
        pl.semaphore_signal(barrier, inc=1, device_id=(peer, t), device_id_type=MESH)

    @pl.when(has_up)
    def _():
        pl.semaphore_signal(barrier, inc=1, device_id=(me, t - 1), device_id_type=MESH)

    @pl.when(has_down)
    def _():
        pl.semaphore_signal(barrier, inc=1, device_id=(me, t + 1), device_id_type=MESH)

    for r in range(0, rows, 8):
        m = [2.0 * medium[0, r : r + 8, k * LANES : (k + 1) * LANES] - 4.0 for k in range(PANELS)]
        for k, v in enumerate(swap_bits(m)):
            index[me, k, rows + r : rows + r + 8, :] = v
    for p in range(2):
        for r in range(0, rows, 8):
            f = [beams[0, p, r : r + 8, k * LANES : (k + 1) * LANES] for k in range(PANELS)]
            for k, v in enumerate(swap_bits(f)):
                field[0, p, k + 1, pad + rows + r : pad + rows + r + 8, :] = v

    zero = jnp.zeros((8, LANES), jnp.float32)

    @pl.loop(0, PANELS + 2)
    def _(k):
        for i in range(2):
            for p in range(2):
                for r in (0, pad + ext):
                    field[i, p, k, r : r + 8, :] = zero
                    work[i, p, k, r : r + 8, :] = zero

    def clear(first):
        @pl.loop(0, PANELS + 2)
        def _(k):
            for i in range(2):
                for p in range(2):
                    for r in range(0, rows, 8):
                        field[i, p, k, pad + first + r : pad + first + r + 8, :] = zero

        @pl.loop(0, secs)
        def _(s):
            for k in range(PANELS):
                for r in range(0, rows, 8):
                    index[s, k, first + r : first + r + 8, :] = zero

    @pl.when(jnp.logical_not(has_up))
    def _():
        clear(0)

    @pl.when(jnp.logical_not(has_down))
    def _():
        clear(2 * rows)

    for r in range(0, ext, 8):
        place = lax.broadcasted_iota(jnp.int32, (8, LANES), 0) + (t * rows + r - rows)
        inside = jnp.logical_and(place >= 0, place < tiles * rows)
        for i, c in enumerate(SCALES):
            scale[i, r : r + 8, :] = jnp.where(inside, jnp.float32(c), jnp.float32(0.0))

    up_edge = (pad + rows, pad + 2 * rows)

    def field_copy(buf, side):
        mine = field.at[buf, :, 1 : PANELS + 1, pad + rows : pad + 2 * rows, :]
        first = pad + (2 * rows if side == 0 else 0)
        theirs = field.at[buf, :, 1 : PANELS + 1, first : first + rows, :]
        return pltpu.make_async_remote_copy(
            src_ref=mine, dst_ref=theirs, send_sem=f_send.at[buf, side], recv_sem=f_recv.at[buf, side],
            device_id=(me, t - 1 if side == 0 else t + 1), device_id_type=MESH)

    def index_copy(s, depth, side):
        first = rows if side == 0 else 2 * rows - depth
        there = 2 * rows if side == 0 else rows - depth
        return pltpu.make_async_remote_copy(
            src_ref=index.at[s, :, first : first + depth, :], dst_ref=index.at[s, :, there : there + depth, :],
            send_sem=h_send.at[s, side], recv_sem=h_recv.at[s, side],
            device_id=(me, t - 1 if side == 0 else t + 1), device_id_type=MESH)

    def both(make, act):
        @pl.when(has_up)
        def _():
            act(make(0))

        @pl.when(has_down)
        def _():
            act(make(1))

    def both_in(make, act):
        @pl.when(has_down)
        def _():
            act(make(0))

        @pl.when(has_up)
        def _():
            act(make(1))

    pl.semaphore_wait(barrier, 4 + has_up.astype(jnp.int32) + has_down.astype(jnp.int32))

    both(lambda side: field_copy(0, side), lambda c: c.start())

    sends = []
    halves = (pl.ds(0, PANELS // 2), pl.ds(PANELS // 2, PANELS // 2))
    every = pl.ds(0, PANELS)

    def send(s, part, peer):
        ref = index.at[s, part, rows : 2 * rows, :]
        copy = pltpu.make_async_remote_copy(
            src_ref=ref, dst_ref=ref, send_sem=m_send.at[len(sends)], recv_sem=m_recv.at[s],
            device_id=(peer, t), device_id_type=MESH)
        copy.start()
        sends.append(copy)

    def arrived(s):
        ref = index.at[s, :, rows : 2 * rows, :]
        pltpu.make_async_remote_copy(
            src_ref=ref, dst_ref=ref, send_sem=m_send.at[0], recv_sem=m_recv.at[s],
            device_id=(me, t), device_id_type=MESH).wait_recv()

    send(me, every, sid(1, 0))
    send(me, every, sid(3, 0))
    send(me, every, sid(0, 1))
    send(me, every, sid(0, 3))
    arrived(sid(3, 0))
    send(sid(3, 0), halves[0], sid(1, 0))
    arrived(sid(1, 0))
    send(sid(1, 0), halves[1], sid(3, 0))
    for da in (3, 1):
        send(sid(da, 0), every, sid(0, 1))
        send(sid(da, 0), every, sid(0, 3))
    arrived(sid(2, 0))
    send(sid(2, 0), every, sid(0, 1))
    send(sid(2, 0), every, sid(0, 3))
    for da in (0, 3, 1, 2):
        arrived(sid(da, 3))
        send(sid(da, 3), halves[0], sid(0, 1))
        arrived(sid(da, 1))
        send(sid(da, 1), halves[1], sid(0, 3))
    for da in (0, 3, 1, 2):
        arrived(sid(da, 2))

    def depth_of(s):
        return rows if s % GROUP < GROUP // 2 else rows // 2

    for s in range(secs):
        both(lambda side, s=s: index_copy(s, depth_of(s), side), lambda c: c.start())

    lane = lax.broadcasted_iota(jnp.int32, (8, LANES), 1)

    def ghosts(ref, first, last):
        for p in range(2):
            for blk in range(first, last):
                r = pad + 8 * blk
                v = ref[p, PANELS, r : r + 8, :]
                left = jnp.where(lane < 16, pltpu.roll(v, 17, 1), pltpu.roll(v, 16, 1))
                ref[p, 0, r : r + 8, :] = jnp.where(lane == 0, 0.0, left)
                v = ref[p, 1, r : r + 8, :]
                right = jnp.where(lane >= LANES - 16, pltpu.roll(v, LANES - 17, 1), pltpu.roll(v, LANES - 16, 1))
                ref[p, PANELS + 1, r : r + 8, :] = jnp.where(lane == LANES - 1, 0.0, right)

    def stage(src, dst, base, s, i, first, last):
        weights = [scale[i, 8 * blk : 8 * blk + 8, :] for blk in range(first, last)]

        @pl.loop(0, PANELS // UNROLL)
        def _(step):
            k0 = step * UNROLL
            for blk in range(first, last):
                r = pad + 8 * blk
                w = weights[blk - first]
                mid = [[src[p, k0 + q, r : r + 8, :] for q in range(UNROLL + 2)] for p in range(2)]
                for u in range(UNROLL):
                    m = index[s, k0 + u, 8 * blk : 8 * blk + 8, :]
                    drive = []
                    for p in range(2):
                        rowsum = src[p, k0 + u + 1, r - 1 : r + 7, :] + src[p, k0 + u + 1, r + 1 : r + 9, :]
                        drive.append(((mid[p][u] + mid[p][u + 2]) + rowsum + m * mid[p][u + 1]) * w)
                    dst[0, k0 + u + 1, r : r + 8, :] = base[0, k0 + u + 1, r : r + 8, :] - drive[1]
                    dst[1, k0 + u + 1, r : r + 8, :] = base[1, k0 + u + 1, r : r + 8, :] + drive[0]

        ghosts(dst, first, last)

    groups = secs // GROUP

    @pl.loop(0, groups)
    def _(g):
        now, later = lax.rem(g, 2), lax.rem(g + 1, 2)
        cur, nxt = field.at[now], field.at[later]
        both_in(lambda side: field_copy(now, side), lambda c: c.wait_recv())
        both(lambda side: field_copy(now, side), lambda c: c.wait_send())
        for j in range(GROUP):
            both_in(lambda side, j=j: index_copy(g * GROUP + j, depth_of(j), side), lambda c: c.wait_recv())
        ghosts(cur, 0, ext // 8)
        for j in range(GROUP):
            s = g * GROUP + j
            for i in range(4):
                n = 4 * j + i + 1
                first, last = n // 8, -(-(ext - n) // 8)
                src = cur if i == 0 else work.at[(i + 1) % 2]
                dst = work.at[i % 2] if i < 3 else (cur if j < GROUP - 1 else nxt)
                stage(src, dst, cur, s, i, first, last)

        @pl.when(g < groups - 1)
        def _():
            both(lambda side: field_copy(later, side), lambda c: c.start())

    final = field.at[groups % 2]
    for p in range(2):
        for r in range(0, rows, 8):
            f = [final[p, k + 1, pad + rows + r : pad + rows + r + 8, :] for k in range(PANELS)]
            for k, v in enumerate(swap_bits(f)):
                out[0, p, r : r + 8, k * LANES : (k + 1) * LANES] = v

    for copy in sends:
        copy.wait_send()
    for s in range(secs):
        both(lambda side, s=s: index_copy(s, depth_of(s), side), lambda c: c.wait_send())


def per_device(tiles, secs, beams, medium):
    rows = medium.shape[1]
    vmem = pl.BlockSpec(memory_space=pltpu.VMEM)
    return pl.pallas_call(
        functools.partial(kernel, tiles, secs),
        out_shape=jax.ShapeDtypeStruct(beams.shape, jnp.float32),
        in_specs=[vmem, vmem],
        out_specs=vmem,
        scratch_shapes=[
            pltpu.VMEM((2, 2, PANELS + 2, 3 * rows + 16, LANES), jnp.float32),
            pltpu.VMEM((2, 2, PANELS + 2, 3 * rows + 16, LANES), jnp.float32),
            pltpu.VMEM((secs, PANELS, 3 * rows, LANES), jnp.float32),
            pltpu.VMEM((4, 3 * rows, LANES), jnp.float32),
            pltpu.SemaphoreType.DMA((20,)),
            pltpu.SemaphoreType.DMA((secs,)),
            pltpu.SemaphoreType.DMA((secs, 2)),
            pltpu.SemaphoreType.DMA((secs, 2)),
            pltpu.SemaphoreType.DMA((2, 2)),
            pltpu.SemaphoreType.DMA((2, 2)),
        ],
        compiler_params=pltpu.CompilerParams(collective_id=0, has_side_effects=True),
        name="propagate",
    )(beams, medium)


def solution(mesh):
    placed = (P("sec", None, "tile", None), P("sec", "tile", None))
    return jax.shard_map(
        functools.partial(per_device, mesh.shape["tile"], mesh.shape["sec"]),
        mesh=mesh,
        in_specs=placed,
        out_specs=P("sec", None, "tile", None),
        check_vma=False,
    )
```

time: 265 us -> 79.2 us (0.30)
  the two profiles are of different devices: /device:TPU:128 before, /device:TPU:97 now
where the time goes in v1:
time: 79.2 us; the launch traced here: 79 us
  Pallas kernels  77.4 us (98%)
  local copies, waits for them, and re-layouts  1.67 us (2%)
    pallas_call x1, Pallas kernels, per_device(): pl.pallas_call(functools.partial(kernel, tiles, secs), out_shape=jax.Shap...  77.4 us
    unnamed x1, local copies, waits for them, and re-layouts  1.67 us

profile of v1, /device:TPU:97, one launch (start us, length us, event | category | flops | bytes accessed | tf_op | source)
XLA Modules:
  0.0 79.0 jit_solution(14181582367263920592)
XLA Ops:
  0.0 77.4 %propagate.1 = f32[1,2,16,2048]{3,2,1,0:T(8,128)} custom-call(f32[1,2,16,2048]{3,2,1,0:T(8,128)} %beams.1, f32[1,16,2048]{2,1,0:T(8,128)} %medium.1), custom_call_target="tpu_custom_call" | custom-call | tf_op jit(solution)/shard_map/propagate/pallas_call | solution.py:273
  77.4 1.7 %copy.4 = f32[1,2,16,2048]{3,2,1,0:T(8,128)} copy(f32[1,2,16,2048]{3,2,1,0:T(8,128)} %propagate.1) | data formatting | bytes 524288

commit v2 on v1

--- a/solution.py
+++ b/solution.py
@@ -62,16 +62,122 @@
     def _():
         pl.semaphore_signal(barrier, inc=1, device_id=(me, t + 1), device_id_type=MESH)
 
+    def field_copy(buf, side):
+        mine = field.at[buf, :, 1 : PANELS + 1, pad + rows : pad + 2 * rows, :]
+        first = pad + (2 * rows if side == 0 else 0)
+        theirs = field.at[buf, :, 1 : PANELS + 1, first : first + rows, :]
+        return pltpu.make_async_remote_copy(
+            src_ref=mine, dst_ref=theirs, send_sem=f_send.at[buf, side], recv_sem=f_recv.at[buf, side],
+            device_id=(me, t - 1 if side == 0 else t + 1), device_id_type=MESH)
+
+    def index_copy(s, depth, side):
+        first = rows if side == 0 else 2 * rows - depth
+        there = 2 * rows if side == 0 else rows - depth
+        return pltpu.make_async_remote_copy(
+            src_ref=index.at[s, :, first : first + depth, :], dst_ref=index.at[s, :, there : there + depth, :],
+            send_sem=h_send.at[s, side], recv_sem=h_recv.at[s, side],
+            device_id=(me, t - 1 if side == 0 else t + 1), device_id_type=MESH)
+
+    def both(make, act):
+        @pl.when(has_up)
+        def _():
+            act(make(0))
+
+        @pl.when(has_down)
+        def _():
+            act(make(1))
+
+    def both_in(make, act):
+        @pl.when(has_down)
+        def _():
+            act(make(0))
+
+        @pl.when(has_up)
+        def _():
+            act(make(1))
+
+    def depth_of(j):
+        return rows - 4 * j
+
+    sends = []
+    halves = (pl.ds(0, PANELS // 2), pl.ds(PANELS // 2, PANELS // 2))
+    every = pl.ds(0, PANELS)
+
+    def send(s, part, peer):
+        ref = index.at[s, part, rows : 2 * rows, :]
+        copy = pltpu.make_async_remote_copy(
+            src_ref=ref, dst_ref=ref, send_sem=m_send.at[len(sends)], recv_sem=m_recv.at[s],
+            device_id=(peer, t), device_id_type=MESH)
+        copy.start()
+        sends.append(copy)
+
+    def edges(s):
+        for j in range(GROUP):
+            @pl.when(lax.rem(s, GROUP) == j)
+            def _():
+                both(lambda side: index_copy(s, depth_of(j), side), lambda c: c.start())
+
+    def arrived(s):
+        ref = index.at[s, :, rows : 2 * rows, :]
+        pltpu.make_async_remote_copy(
+            src_ref=ref, dst_ref=ref, send_sem=m_send.at[0], recv_sem=m_recv.at[s],
+            device_id=(me, t), device_id_type=MESH).wait_recv()
+
     for r in range(0, rows, 8):
         m = [2.0 * medium[0, r : r + 8, k * LANES : (k + 1) * LANES] - 4.0 for k in range(PANELS)]
         for k, v in enumerate(swap_bits(m)):
             index[me, k, rows + r : rows + r + 8, :] = v
+    pl.semaphore_wait(barrier, 4 + has_up.astype(jnp.int32) + has_down.astype(jnp.int32))
+    send(me, every, sid(1, 0))
+    send(me, every, sid(3, 0))
+    send(me, every, sid(0, 1))
+    send(me, every, sid(0, 3))
     for p in range(2):
         for r in range(0, rows, 8):
             f = [beams[0, p, r : r + 8, k * LANES : (k + 1) * LANES] for k in range(PANELS)]
             for k, v in enumerate(swap_bits(f)):
                 field[0, p, k + 1, pad + rows + r : pad + rows + r + 8, :] = v
 
+    both(lambda side: field_copy(0, side), lambda c: c.start())
+    lane = lax.broadcasted_iota(jnp.int32, (8, LANES), 1)
+
+    def before_first(v):
+        left = jnp.where(lane < 16, pltpu.roll(v, 17, 1), pltpu.roll(v, 16, 1))
+        return jnp.where(lane == 0, 0.0, left)
+
+    def after_last(v):
+        right = jnp.where(lane >= LANES - 16, pltpu.roll(v, LANES - 17, 1), pltpu.roll(v, LANES - 16, 1))
+        return jnp.where(lane == LANES - 1, 0.0, right)
+
+    def ghosts(ref, blocks):
+        for blk in blocks:
+            for p in range(2):
+                r = pad + 8 * blk
+                ref[p, 0, r : r + 8, :] = before_first(ref[p, PANELS, r : r + 8, :])
+                ref[p, PANELS + 1, r : r + 8, :] = after_last(ref[p, 1, r : r + 8, :])
+
+    def stage(src, dst, base, s, i, first, last):
+        for k0 in (PANELS - UNROLL,) + tuple(range(0, PANELS - UNROLL, UNROLL)):
+            for blk in range(first, last):
+                r = pad + 8 * blk
+                w = scale[i, 8 * blk : 8 * blk + 8, :]
+                mid = [[src[p, k0 + q, r : r + 8, :] for q in range(UNROLL + 2)] for p in range(2)]
+                for u in range(UNROLL):
+                    k = k0 + u
+                    m = index[s, k, 8 * blk : 8 * blk + 8, :]
+                    drive = []
+                    for p in range(2):
+                        rowsum = src[p, k + 1, r - 1 : r + 7, :] + src[p, k + 1, r + 1 : r + 9, :]
+                        drive.append(((mid[p][u] + mid[p][u + 2]) + rowsum + m * mid[p][u + 1]) * w)
+                    new = (base[0, k + 1, r : r + 8, :] - drive[1], base[1, k + 1, r : r + 8, :] + drive[0])
+                    for p in range(2):
+                        dst[p, k + 1, r : r + 8, :] = new[p]
+                        if k == 0:
+                            dst[p, PANELS + 1, r : r + 8, :] = after_last(new[p])
+                        if k == PANELS - 1:
+                            dst[p, 0, r : r + 8, :] = before_first(new[p])
+
+    ghosts(field.at[0], range(rows // 8, 2 * rows // 8))
     zero = jnp.zeros((8, LANES), jnp.float32)
 
     @pl.loop(0, PANELS + 2)
@@ -110,68 +216,7 @@
         for i, c in enumerate(SCALES):
             scale[i, r : r + 8, :] = jnp.where(inside, jnp.float32(c), jnp.float32(0.0))
 
-    up_edge = (pad + rows, pad + 2 * rows)
-
-    def field_copy(buf, side):
-        mine = field.at[buf, :, 1 : PANELS + 1, pad + rows : pad + 2 * rows, :]
-        first = pad + (2 * rows if side == 0 else 0)
-        theirs = field.at[buf, :, 1 : PANELS + 1, first : first + rows, :]
-        return pltpu.make_async_remote_copy(
-            src_ref=mine, dst_ref=theirs, send_sem=f_send.at[buf, side], recv_sem=f_recv.at[buf, side],
-            device_id=(me, t - 1 if side == 0 else t + 1), device_id_type=MESH)
-
-    def index_copy(s, depth, side):
-        first = rows if side == 0 else 2 * rows - depth
-        there = 2 * rows if side == 0 else rows - depth
-        return pltpu.make_async_remote_copy(
-            src_ref=index.at[s, :, first : first + depth, :], dst_ref=index.at[s, :, there : there + depth, :],
-            send_sem=h_send.at[s, side], recv_sem=h_recv.at[s, side],
-            device_id=(me, t - 1 if side == 0 else t + 1), device_id_type=MESH)
-
-    def both(make, act):
-        @pl.when(has_up)
-        def _():
-            act(make(0))
-
-        @pl.when(has_down)
-        def _():
-            act(make(1))
-
-    def both_in(make, act):
-        @pl.when(has_down)
-        def _():
-            act(make(0))
-
-        @pl.when(has_up)
-        def _():
-            act(make(1))
-
-    pl.semaphore_wait(barrier, 4 + has_up.astype(jnp.int32) + has_down.astype(jnp.int32))
-
-    both(lambda side: field_copy(0, side), lambda c: c.start())
-
-    sends = []
-    halves = (pl.ds(0, PANELS // 2), pl.ds(PANELS // 2, PANELS // 2))
-    every = pl.ds(0, PANELS)
-
-    def send(s, part, peer):
-        ref = index.at[s, part, rows : 2 * rows, :]
-        copy = pltpu.make_async_remote_copy(
-            src_ref=ref, dst_ref=ref, send_sem=m_send.at[len(sends)], recv_sem=m_recv.at[s],
-            device_id=(peer, t), device_id_type=MESH)
-        copy.start()
-        sends.append(copy)
-
-    def arrived(s):
-        ref = index.at[s, :, rows : 2 * rows, :]
-        pltpu.make_async_remote_copy(
-            src_ref=ref, dst_ref=ref, send_sem=m_send.at[0], recv_sem=m_recv.at[s],
-            device_id=(me, t), device_id_type=MESH).wait_recv()
-
-    send(me, every, sid(1, 0))
-    send(me, every, sid(3, 0))
-    send(me, every, sid(0, 1))
-    send(me, every, sid(0, 3))
+    edges(me)
     arrived(sid(3, 0))
     send(sid(3, 0), halves[0], sid(1, 0))
     arrived(sid(1, 0))
@@ -179,56 +224,21 @@
     for da in (3, 1):
         send(sid(da, 0), every, sid(0, 1))
         send(sid(da, 0), every, sid(0, 3))
+        edges(sid(da, 0))
     arrived(sid(2, 0))
     send(sid(2, 0), every, sid(0, 1))
     send(sid(2, 0), every, sid(0, 3))
+    edges(sid(2, 0))
     for da in (0, 3, 1, 2):
         arrived(sid(da, 3))
         send(sid(da, 3), halves[0], sid(0, 1))
         arrived(sid(da, 1))
         send(sid(da, 1), halves[1], sid(0, 3))
+        edges(sid(da, 3))
+        edges(sid(da, 1))
     for da in (0, 3, 1, 2):
         arrived(sid(da, 2))
-
-    def depth_of(s):
-        return rows if s % GROUP < GROUP // 2 else rows // 2
-
-    for s in range(secs):
-        both(lambda side, s=s: index_copy(s, depth_of(s), side), lambda c: c.start())
-
-    lane = lax.broadcasted_iota(jnp.int32, (8, LANES), 1)
-
-    def ghosts(ref, first, last):
-        for p in range(2):
-            for blk in range(first, last):
-                r = pad + 8 * blk
-                v = ref[p, PANELS, r : r + 8, :]
-                left = jnp.where(lane < 16, pltpu.roll(v, 17, 1), pltpu.roll(v, 16, 1))
-                ref[p, 0, r : r + 8, :] = jnp.where(lane == 0, 0.0, left)
-                v = ref[p, 1, r : r + 8, :]
-                right = jnp.where(lane >= LANES - 16, pltpu.roll(v, LANES - 17, 1), pltpu.roll(v, LANES - 16, 1))
-                ref[p, PANELS + 1, r : r + 8, :] = jnp.where(lane == LANES - 1, 0.0, right)
-
-    def stage(src, dst, base, s, i, first, last):
-        weights = [scale[i, 8 * blk : 8 * blk + 8, :] for blk in range(first, last)]
-
-        @pl.loop(0, PANELS // UNROLL)
-        def _(step):
-            k0 = step * UNROLL
-            for blk in range(first, last):
-                r = pad + 8 * blk
-                w = weights[blk - first]
-                mid = [[src[p, k0 + q, r : r + 8, :] for q in range(UNROLL + 2)] for p in range(2)]
-                for u in range(UNROLL):
-                    m = index[s, k0 + u, 8 * blk : 8 * blk + 8, :]
-                    drive = []
-                    for p in range(2):
-                        rowsum = src[p, k0 + u + 1, r - 1 : r + 7, :] + src[p, k0 + u + 1, r + 1 : r + 9, :]
-                        drive.append(((mid[p][u] + mid[p][u + 2]) + rowsum + m * mid[p][u + 1]) * w)
-                    dst[0, k0 + u + 1, r : r + 8, :] = base[0, k0 + u + 1, r : r + 8, :] - drive[1]
-                    dst[1, k0 + u + 1, r : r + 8, :] = base[1, k0 + u + 1, r : r + 8, :] + drive[0]
-
-        ghosts(dst, first, last)
+        edges(sid(da, 2))
 
     groups = secs // GROUP
 
@@ -238,11 +248,10 @@
         cur, nxt = field.at[now], field.at[later]
         both_in(lambda side: field_copy(now, side), lambda c: c.wait_recv())
         both(lambda side: field_copy(now, side), lambda c: c.wait_send())
-        for j in range(GROUP):
-            both_in(lambda side, j=j: index_copy(g * GROUP + j, depth_of(j), side), lambda c: c.wait_recv())
-        ghosts(cur, 0, ext // 8)
+        ghosts(cur, [blk for blk in range(ext // 8) if not rows <= 8 * blk < 2 * rows])
         for j in range(GROUP):
             s = g * GROUP + j
+            both_in(lambda side: index_copy(s, depth_of(j), side), lambda c: c.wait_recv())
             for i in range(4):
                 n = 4 * j + i + 1
                 first, last = n // 8, -(-(ext - n) // 8)
@@ -264,7 +273,7 @@
     for copy in sends:
         copy.wait_send()
     for s in range(secs):
-        both(lambda side, s=s: index_copy(s, depth_of(s), side), lambda c: c.wait_send())
+        both(lambda side, s=s: index_copy(s, depth_of(s % GROUP), side), lambda c: c.wait_send())
 
 
 def per_device(tiles, secs, beams, medium):

time: 79.2 us -> 64.1 us (0.81)
  the two profiles are of different devices: /device:TPU:97 before, /device:TPU:245 now
where the time goes in v2:
time: 64.1 us; the launch traced here: 64 us
  Pallas kernels  62.3 us (97%)
  local copies, waits for them, and re-layouts  1.67 us (3%)
    pallas_call x1, Pallas kernels, per_device(): pl.pallas_call(functools.partial(kernel, tiles, secs), out_shape=jax.Shap...  62.3 us
    unnamed x1, local copies, waits for them, and re-layouts  1.67 us

profile of v2, /device:TPU:245, one launch (start us, length us, event | category | flops | bytes accessed | tf_op | source)
XLA Modules:
  0.0 64.0 jit_solution(7370437083935493602)
XLA Ops:
  0.0 62.3 %propagate.1 = f32[1,2,16,2048]{3,2,1,0:T(8,128)} custom-call(f32[1,2,16,2048]{3,2,1,0:T(8,128)} %beams.1, f32[1,16,2048]{2,1,0:T(8,128)} %medium.1), custom_call_target="tpu_custom_call" | custom-call | tf_op jit(solution)/shard_map/propagate/pallas_call | solution.py:282
  62.3 1.7 %copy.4 = f32[1,2,16,2048]{3,2,1,0:T(8,128)} copy(f32[1,2,16,2048]{3,2,1,0:T(8,128)} %propagate.1) | data formatting | bytes 524288

commit v3 on v2

--- a/solution.py
+++ b/solution.py
@@ -33,7 +33,7 @@
     return tiles
 
 
-def kernel(tiles, secs, beams, medium, out, field, work, index, scale, m_send, m_recv, h_send, h_recv, f_send, f_recv):
+def kernel(tiles, secs, beams, medium, out, field, work_a, work_b, index, scale, m_send, m_recv, h_send, h_recv, f_send, f_recv):
     rows = medium.shape[1]
     ext = 3 * rows
     pad = 8
@@ -116,6 +116,18 @@
             @pl.when(lax.rem(s, GROUP) == j)
             def _():
                 both(lambda side: index_copy(s, depth_of(j), side), lambda c: c.start())
+
+    def first_edges(s):
+        for j in range(GROUP):
+            @pl.when(s == j)
+            def _():
+                both(lambda side: index_copy(j, depth_of(j), side), lambda c: c.start())
+
+    def later_edges(g):
+        for j in range(GROUP):
+            @pl.when(g * (1 - odd) + j * odd != b)
+            def _():
+                both(lambda side: index_copy(g * GROUP + j, depth_of(j), side), lambda c: c.start())
 
     def arrived(s):
         ref = index.at[s, :, rows : 2 * rows, :]
@@ -186,7 +198,7 @@
             for p in range(2):
                 for r in (0, pad + ext):
                     field[i, p, k, r : r + 8, :] = zero
-                    work[i, p, k, r : r + 8, :] = zero
+                    (work_a, work_b)[i][p, k, r : r + 8, :] = zero
 
     def clear(first):
         @pl.loop(0, PANELS + 2)
@@ -234,11 +246,11 @@
         send(sid(da, 3), halves[0], sid(0, 1))
         arrived(sid(da, 1))
         send(sid(da, 1), halves[1], sid(0, 3))
-        edges(sid(da, 3))
-        edges(sid(da, 1))
+        first_edges(sid(da, 3))
+        first_edges(sid(da, 1))
     for da in (0, 3, 1, 2):
         arrived(sid(da, 2))
-        edges(sid(da, 2))
+        first_edges(sid(da, 2))
 
     groups = secs // GROUP
 
@@ -248,6 +260,11 @@
         cur, nxt = field.at[now], field.at[later]
         both_in(lambda side: field_copy(now, side), lambda c: c.wait_recv())
         both(lambda side: field_copy(now, side), lambda c: c.wait_send())
+
+        @pl.when(g < groups - 1)
+        def _():
+            later_edges(g + 1)
+
         ghosts(cur, [blk for blk in range(ext // 8) if not rows <= 8 * blk < 2 * rows])
         for j in range(GROUP):
             s = g * GROUP + j
@@ -255,8 +272,8 @@
             for i in range(4):
                 n = 4 * j + i + 1
                 first, last = n // 8, -(-(ext - n) // 8)
-                src = cur if i == 0 else work.at[(i + 1) % 2]
-                dst = work.at[i % 2] if i < 3 else (cur if j < GROUP - 1 else nxt)
+                src = cur if i == 0 else (work_a, work_b)[(i + 1) % 2]
+                dst = (work_a, work_b)[i % 2] if i < 3 else (cur if j < GROUP - 1 else nxt)
                 stage(src, dst, cur, s, i, first, last)
 
         @pl.when(g < groups - 1)
@@ -286,7 +303,8 @@
         out_specs=vmem,
         scratch_shapes=[
             pltpu.VMEM((2, 2, PANELS + 2, 3 * rows + 16, LANES), jnp.float32),
-            pltpu.VMEM((2, 2, PANELS + 2, 3 * rows + 16, LANES), jnp.float32),
+            pltpu.VMEM((2, PANELS + 2, 3 * rows + 16, LANES), jnp.float32),
+            pltpu.VMEM((2, PANELS + 2, 3 * rows + 16, LANES), jnp.float32),
             pltpu.VMEM((secs, PANELS, 3 * rows, LANES), jnp.float32),
             pltpu.VMEM((4, 3 * rows, LANES), jnp.float32),
             pltpu.SemaphoreType.DMA((20,)),

time: 64.1 us -> 61.7 us (0.963)
  the two profiles are of different devices: /device:TPU:245 before, /device:TPU:97 now
where the time goes in v3:
time: 61.7 us; the launch traced here: 61.5 us
  Pallas kernels  59.9 us (97%)
  local copies, waits for them, and re-layouts  1.67 us (3%)
    pallas_call x1, Pallas kernels, per_device(): pl.pallas_call(functools.partial(kernel, tiles, secs), out_shape=jax.Shap...  59.9 us
    unnamed x1, local copies, waits for them, and re-layouts  1.67 us

profile of v3, /device:TPU:97, one launch (start us, length us, event | category | flops | bytes accessed | tf_op | source)
XLA Modules:
  0.0 61.5 jit_solution(4985449482049218149)
XLA Ops:
  0.0 59.9 %propagate.1 = f32[1,2,16,2048]{3,2,1,0:T(8,128)} custom-call(f32[1,2,16,2048]{3,2,1,0:T(8,128)} %beams.1, f32[1,16,2048]{2,1,0:T(8,128)} %medium.1), custom_call_target="tpu_custom_call" | custom-call | tf_op jit(solution)/shard_map/propagate/pallas_call | solution.py:299
  59.9 1.7 %copy.4 = f32[1,2,16,2048]{3,2,1,0:T(8,128)} copy(f32[1,2,16,2048]{3,2,1,0:T(8,128)} %propagate.1) | data formatting | bytes 524288

commit v4 on v3

--- a/solution.py
+++ b/solution.py
@@ -118,10 +118,12 @@
                 both(lambda side: index_copy(s, depth_of(j), side), lambda c: c.start())
 
     def first_edges(s):
-        for j in range(GROUP):
-            @pl.when(s == j)
-            def _():
-                both(lambda side: index_copy(j, depth_of(j), side), lambda c: c.start())
+        @pl.when(s < GROUP)
+        def _():
+            for j in range(GROUP):
+                @pl.when(s == j)
+                def _():
+                    both(lambda side: index_copy(j, depth_of(j), side), lambda c: c.start())
 
     def later_edges(g):
         for j in range(GROUP):
@@ -169,7 +171,9 @@
                 ref[p, PANELS + 1, r : r + 8, :] = after_last(ref[p, 1, r : r + 8, :])
 
     def stage(src, dst, base, s, i, first, last):
-        for k0 in (PANELS - UNROLL,) + tuple(range(0, PANELS - UNROLL, UNROLL)):
+        ends = (PANELS - UNROLL, 0)
+        inner = tuple(range(UNROLL, PANELS - UNROLL, UNROLL))
+        for k0 in (inner + ends if i == 0 and first == 0 and base is src else ends + inner):
             for blk in range(first, last):
                 r = pad + 8 * blk
                 w = scale[i, 8 * blk : 8 * blk + 8, :]
@@ -237,17 +241,22 @@
         send(sid(da, 0), every, sid(0, 1))
         send(sid(da, 0), every, sid(0, 3))
         edges(sid(da, 0))
-    arrived(sid(2, 0))
-    send(sid(2, 0), every, sid(0, 1))
-    send(sid(2, 0), every, sid(0, 3))
-    edges(sid(2, 0))
-    for da in (0, 3, 1, 2):
+
+    def relay(da):
         arrived(sid(da, 3))
         send(sid(da, 3), halves[0], sid(0, 1))
         arrived(sid(da, 1))
         send(sid(da, 1), halves[1], sid(0, 3))
         first_edges(sid(da, 3))
         first_edges(sid(da, 1))
+
+    relay(0)
+    arrived(sid(2, 0))
+    send(sid(2, 0), every, sid(0, 1))
+    send(sid(2, 0), every, sid(0, 3))
+    edges(sid(2, 0))
+    for da in (3, 1, 2):
+        relay(da)
     for da in (0, 3, 1, 2):
         arrived(sid(da, 2))
         first_edges(sid(da, 2))
@@ -260,15 +269,14 @@
         cur, nxt = field.at[now], field.at[later]
         both_in(lambda side: field_copy(now, side), lambda c: c.wait_recv())
         both(lambda side: field_copy(now, side), lambda c: c.wait_send())
-
-        @pl.when(g < groups - 1)
-        def _():
-            later_edges(g + 1)
-
-        ghosts(cur, [blk for blk in range(ext // 8) if not rows <= 8 * blk < 2 * rows])
         for j in range(GROUP):
             s = g * GROUP + j
             both_in(lambda side: index_copy(s, depth_of(j), side), lambda c: c.wait_recv())
+            if j == 0:
+                @pl.when(g == 0)
+                def _():
+                    later_edges(1)
+                ghosts(cur, [blk for blk in range(ext // 8) if not rows <= 8 * blk < 2 * rows])
             for i in range(4):
                 n = 4 * j + i + 1
                 first, last = n // 8, -(-(ext - n) // 8)
@@ -280,6 +288,18 @@
         def _():
             both(lambda side: field_copy(later, side), lambda c: c.start())
 
+            @pl.when(g < groups - 2)
+            def _():
+                later_edges(g + 2)
+
+            @pl.when(g == 0)
+            def _():
+                for copy in sends:
+                    copy.wait_send()
+
+            for j in range(GROUP):
+                both(lambda side: index_copy(g * GROUP + j, depth_of(j), side), lambda c: c.wait_send())
+
     final = field.at[groups % 2]
     for p in range(2):
         for r in range(0, rows, 8):
@@ -287,9 +307,7 @@
             for k, v in enumerate(swap_bits(f)):
                 out[0, p, r : r + 8, k * LANES : (k + 1) * LANES] = v
 
-    for copy in sends:
-        copy.wait_send()
-    for s in range(secs):
+    for s in range(secs - GROUP, secs):
         both(lambda side, s=s: index_copy(s, depth_of(s % GROUP), side), lambda c: c.wait_send())
 
 

time: 61.7 us -> 61.6 us (level)
  no operation moved by 1% of the time
where the time goes in v4:
time: 61.6 us; the launch traced here: 61.4 us
  Pallas kernels  59.7 us (97%)
  local copies, waits for them, and re-layouts  1.67 us (3%)
    pallas_call x1, Pallas kernels, per_device(): pl.pallas_call(functools.partial(kernel, tiles, secs), out_shape=jax.Shap...  59.7 us
    unnamed x1, local copies, waits for them, and re-layouts  1.67 us

profile of v4, /device:TPU:97, one launch (start us, length us, event | category | flops | bytes accessed | tf_op | source)
XLA Modules:
  0.0 61.4 jit_solution(11740333152158333086)
XLA Ops:
  0.0 59.7 %propagate.1 = f32[1,2,16,2048]{3,2,1,0:T(8,128)} custom-call(f32[1,2,16,2048]{3,2,1,0:T(8,128)} %beams.1, f32[1,16,2048]{2,1,0:T(8,128)} %medium.1), custom_call_target="tpu_custom_call" | custom-call | tf_op jit(solution)/shard_map/propagate/pallas_call | solution.py:317
  59.7 1.7 %copy.4 = f32[1,2,16,2048]{3,2,1,0:T(8,128)} copy(f32[1,2,16,2048]{3,2,1,0:T(8,128)} %propagate.1) | data formatting | bytes 524288
